TPU v7x, 32 devices: a whole 2x2x4 slice. The times are simulated.
32 devices in a mesh: row: 4 (over y, x), col: 8 (over z, core).
Axes of the slice: x: 2, y: 2, z: 4, core: 2. Of those that a mesh axis runs over, the one named last changes fastest.
Arguments:
- homolog_stack: bfloat16 [128, 128, 256], P(('row', 'col')), may hold values from -6 to 6
- per_amino_features: bfloat16 [128, 256], P(('row', 'col')), may hold values from -6 to 6
- asking_matrix: bfloat16 [256, 256], replicated, may hold values from -24 to 24
- lookup_matrix: bfloat16 [256, 256], replicated, may hold values from -0.375 to 0.375
- content_matrix: bfloat16 [256, 256], replicated, may hold values from -0.375 to 0.375
- sigmoid_scaling_matrix: bfloat16 [256, 256], replicated, may hold values from -0.375 to 0.375
- attention_result_matrix: bfloat16 [256, 256], replicated, may hold values from -0.375 to 0.375
- stack_transition_expand_matrix: bfloat16 [256, 1024], replicated, may hold values from -0.375 to 0.375
- stack_transition_shrink_matrix: bfloat16 [1024, 256], replicated, may hold values from -0.1875 to 0.1875
- former_factor_matrix: bfloat16 [256, 32], replicated, may hold values from -0.375 to 0.375
- latter_factor_matrix: bfloat16 [256, 32], replicated, may hold values from -0.375 to 0.375
- factor_mean_projection: bfloat16 [1024, 128], replicated, may hold values from -1.1953125 to 1.1953125
- row_amino_embedding: bfloat16 [256, 128], replicated, may hold values from -0.375 to 0.375
- column_amino_embedding: bfloat16 [256, 128], replicated, may hold values from -0.375 to 0.375
- offset_embedding_matrix: bfloat16 [65, 128], replicated, may hold values from -3 to 3
- grid_transition_expand: bfloat16 [128, 512], replicated, may hold values from -0.5 to 0.5
- grid_transition_shrink: bfloat16 [512, 128], replicated, may hold values from -0.25 to 0.25
- distance_bins_matrix: bfloat16 [128, 64], replicated, may hold values from -0.5 to 0.5
Outputs:
- alignment_output: bfloat16 [128, 128, 256], P(None, ('row', 'col'))
- pair_output: bfloat16 [128, 128, 128], P('row', 'col')
- distogram: bfloat16 [128, 128, 64], P('row', 'col')
All inputs are finite; a program needn't handle non-finite values.
Results may differ from a plain program's by a relative error of at most 0.011.
The roundings to bfloat16 on the way count: a program that leaves them out, or rounds other values in their place, can miss the bound.
Values may be sent and summed in bfloat16 or wider, within the bound.
No kernel may reach another device: no remote copies, remote signals or barrier semaphores. Data moves between devices by JAX's collectives and lax.ppermute only.
A program may use at most 256 MiB of HBM per device.

v0:
```python
import math
import jax
import jax.numpy as jnp
from jax import lax
from jax.sharding import PartitionSpec as P

HEADS = 8
HEAD = 32
CLIP = 32


def spread_2(block, axis, source):
    block = jnp.where(lax.axis_index(axis) == source, block, jnp.zeros_like(block))
    return lax.psum(block, axis)


def standardize_features(values):
    middle = jnp.mean(values, -1, keepdims=True)
    centred = values - middle
    spread = jnp.mean(centred * centred, -1, keepdims=True)
    return centred * lax.rsqrt(spread + 1e-05)


def alignment_layer(
    block_piece,
    asking_matrix,
    lookup_matrix,
    content_matrix,
    sigmoid_scaling_matrix,
    attention_result_matrix,
    stack_transition_expand_matrix,
    stack_transition_shrink_matrix,
):
    count_seq, count_res, feature_width = block_piece.shape
    start = block_piece.astype(jnp.float32).reshape(-1, feature_width)
    standardized = standardize_features(start).astype(jnp.bfloat16)
    query = jnp.dot(standardized, asking_matrix, preferred_element_type=jnp.float32).astype(
        jnp.bfloat16
    )
    key_rows = jnp.dot(standardized, lookup_matrix, preferred_element_type=jnp.float32).astype(
        jnp.bfloat16
    )
    value_rows = jnp.dot(standardized, content_matrix, preferred_element_type=jnp.float32).astype(
        jnp.bfloat16
    )
    gate = jax.nn.sigmoid(
        jnp.dot(standardized, sigmoid_scaling_matrix, preferred_element_type=jnp.float32)
    )
    query = query.reshape(count_seq, count_res, HEADS, HEAD)
    key_rows = key_rows.reshape(count_seq, count_res, HEADS, HEAD)
    value_rows = value_rows.reshape(count_seq, count_res, HEADS, HEAD)
    scores = jnp.einsum(
        "sihd,tihd->ihst", query, key_rows, preferred_element_type=jnp.float32
    ) / math.sqrt(HEAD)
    weights = jax.nn.softmax(scores, -1).astype(jnp.bfloat16)
    attended = jnp.einsum(
        "ihst,tihd->sihd", weights, value_rows, preferred_element_type=jnp.float32
    ).reshape(-1, feature_width)
    mixed = (attended * gate).astype(jnp.bfloat16)
    first_part = start + jnp.dot(mixed, attention_result_matrix, preferred_element_type=jnp.float32)
    hidden_units = jax.nn.relu(
        jnp.dot(
            standardize_features(first_part).astype(jnp.bfloat16),
            stack_transition_expand_matrix,
            preferred_element_type=jnp.float32,
        )
    ).astype(jnp.bfloat16)
    second_part = first_part + jnp.dot(
        hidden_units, stack_transition_shrink_matrix, preferred_element_type=jnp.float32
    )
    return second_part.reshape(count_seq, count_res, feature_width)


def pair_block(
    a_u,
    b_v,
    left_u,
    right_v,
    start_u,
    start_v,
    offset_embedding_matrix,
    factor_mean_projection,
    grid_transition_expand,
    grid_transition_shrink,
    distance_bins_matrix,
):
    count_seq, count_u, factor = a_u.shape
    count_v = b_v.shape[1]
    feature_width = left_u.shape[1]
    step_rows = max(1, min(count_u, 1024 // count_v))
    tile_collection = count_u // step_rows
    a_blocks = a_u.reshape(count_seq, tile_collection, step_rows, factor).transpose(1, 0, 2, 3)
    left_blocks = left_u.reshape(tile_collection, step_rows, feature_width)
    flat_v = b_v.reshape(count_seq, count_v * factor)
    columns = start_v + jnp.arange(count_v, dtype=jnp.int32)
    bins = jnp.arange(2 * CLIP + 1, dtype=jnp.int32)

    def one_block(inputs):
        a_blk, left_blk, index = inputs
        outer = lax.dot_general(
            a_blk.reshape(count_seq, step_rows * factor),
            flat_v,
            (((0,), (0,)), ((), ())),
            preferred_element_type=jnp.float32,
        )
        outer = (
            outer.reshape(step_rows, factor, count_v, factor)
            .transpose(0, 2, 1, 3)
            .reshape(step_rows * count_v, factor * factor)
        )
        outer = (outer / count_seq).astype(jnp.bfloat16)
        projected = jnp.dot(outer, factor_mean_projection, preferred_element_type=jnp.float32)
        rows_here = start_u + index * step_rows + jnp.arange(step_rows, dtype=jnp.int32)
        offset = jnp.clip(columns[None, :] - rows_here[:, None], -CLIP, CLIP) + CLIP
        onehot = (offset[:, :, None] == bins).astype(jnp.bfloat16).reshape(-1, 2 * CLIP + 1)
        relative = jnp.dot(onehot, offset_embedding_matrix, preferred_element_type=jnp.float32)
        embedded = (
            left_blk.astype(jnp.float32)[:, None, :] + right_v.astype(jnp.float32)[None, :, :]
        ).reshape(-1, feature_width)
        start_pair = embedded + relative + projected
        hidden_units = jax.nn.relu(
            jnp.dot(
                standardize_features(start_pair).astype(jnp.bfloat16),
                grid_transition_expand,
                preferred_element_type=jnp.float32,
            )
        ).astype(jnp.bfloat16)
        final = start_pair + jnp.dot(
            hidden_units, grid_transition_shrink, preferred_element_type=jnp.float32
        )
        rounded = final.astype(jnp.bfloat16)
        logits = jnp.dot(rounded, distance_bins_matrix, preferred_element_type=jnp.float32)
        return (
            rounded.reshape(step_rows, count_v, feature_width),
            logits.reshape(step_rows, count_v, -1),
        )

    pairs, logits = lax.map(
        one_block, (a_blocks, left_blocks, jnp.arange(tile_collection, dtype=jnp.int32))
    )
    return (pairs.reshape(count_u, count_v, feature_width), logits.reshape(count_u, count_v, -1))


def shards(
    homolog_stack,
    per_amino_features,
    asking_matrix,
    lookup_matrix,
    content_matrix,
    sigmoid_scaling_matrix,
    attention_result_matrix,
    stack_transition_expand_matrix,
    stack_transition_shrink_matrix,
    former_factor_matrix,
    latter_factor_matrix,
    factor_mean_projection,
    row_amino_embedding,
    column_amino_embedding,
    offset_embedding_matrix,
    grid_transition_expand,
    grid_transition_shrink,
    distance_bins_matrix,
):
    row_count = lax.axis_size("row")
    col_count = lax.axis_size("col")
    whole_mesh_axes = row_count * col_count
    homolog_shard_here, amino_collection, feature_width = homolog_stack.shape
    amino_shard_here = amino_collection // whole_mesh_axes
    fragment_collection = homolog_stack.reshape(
        1, homolog_shard_here, whole_mesh_axes, amino_shard_here, feature_width
    )
    moved = lax.all_to_all(
        fragment_collection, ("row", "col"), split_axis=2, concat_axis=0, tiled=True
    )
    local_part = moved.reshape(-1, amino_shard_here, feature_width)
    count_seq = local_part.shape[0]
    refreshed_stack = alignment_layer(
        local_part,
        asking_matrix,
        lookup_matrix,
        content_matrix,
        sigmoid_scaling_matrix,
        attention_result_matrix,
        stack_transition_expand_matrix,
        stack_transition_shrink_matrix,
    )
    alignment_output = refreshed_stack.astype(jnp.bfloat16)
    standardized = (
        standardize_features(refreshed_stack).astype(jnp.bfloat16).reshape(-1, feature_width)
    )
    left_opm = (
        jnp.dot(standardized, former_factor_matrix, preferred_element_type=jnp.float32)
        .astype(jnp.bfloat16)
        .reshape(count_seq, amino_shard_here, -1)
    )
    right_opm = (
        jnp.dot(standardized, latter_factor_matrix, preferred_element_type=jnp.float32)
        .astype(jnp.bfloat16)
        .reshape(count_seq, amino_shard_here, -1)
    )
    left_pair = jnp.dot(
        per_amino_features, row_amino_embedding, preferred_element_type=jnp.float32
    ).astype(jnp.bfloat16)
    right_pair = jnp.dot(
        per_amino_features, column_amino_embedding, preferred_element_type=jnp.float32
    ).astype(jnp.bfloat16)
    row_len = amino_collection // row_count
    col_len = amino_collection // col_count
    ratio = col_count // row_count
    row_a, row_b, row_left, row_right = (
        lax.all_gather(left_opm, "col", axis=1, tiled=True),
        lax.all_gather(right_opm, "col", axis=1, tiled=True),
        lax.all_gather(left_pair, "col", axis=0, tiled=True),
        lax.all_gather(right_pair, "col", axis=0, tiled=True),
    )
    offset = lax.axis_index("col") % ratio * col_len
    part_a = lax.dynamic_slice_in_dim(row_a, offset, col_len, 1)
    part_b = lax.dynamic_slice_in_dim(row_b, offset, col_len, 1)
    part_left = lax.dynamic_slice_in_dim(row_left, offset, col_len, 0)
    part_right = lax.dynamic_slice_in_dim(row_right, offset, col_len, 0)
    col_a, col_b, col_left, col_right = (
        spread_2(part_a, "row", lax.axis_index("col") // ratio),
        spread_2(part_b, "row", lax.axis_index("col") // ratio),
        spread_2(part_left, "row", lax.axis_index("col") // ratio),
        spread_2(part_right, "row", lax.axis_index("col") // ratio),
    )
    row_start = lax.axis_index("row") * row_len
    col_start = lax.axis_index("col") * col_len
    pair_output, logits = pair_block(
        row_a,
        col_b,
        row_left,
        col_right,
        row_start,
        col_start,
        offset_embedding_matrix,
        factor_mean_projection,
        grid_transition_expand,
        grid_transition_shrink,
        distance_bins_matrix,
    )
    ignored, mirror = pair_block(
        col_a,
        row_b,
        col_left,
        row_right,
        col_start,
        row_start,
        offset_embedding_matrix,
        factor_mean_projection,
        grid_transition_expand,
        grid_transition_shrink,
        distance_bins_matrix,
    )
    distogram = (logits + mirror.transpose(1, 0, 2)).astype(jnp.bfloat16)
    return (alignment_output, pair_output, distogram)


def solution(mesh):
    placed = (
        P(("row", "col"), None, None),
        P(("row", "col"), None),
        P(),
        P(),
        P(),
        P(),
        P(),
        P(),
        P(),
        P(),
        P(),
        P(),
        P(),
        P(),
        P(),
        P(),
        P(),
        P(),
    )
    return jax.shard_map(
        shards,
        mesh=mesh,
        in_specs=placed,
        out_specs=(P(None, ("row", "col"), None), P("row", "col", None), P("row", "col", None)),
        check_vma=False,
    )
```

profile of v0, /device:TPU:0, one launch (start us, length us, event | category | flops | bytes accessed | tf_op | source)
XLA Modules:
  0.0 171.2 jit_solution(15490688881708692075)
XLA Ops:
  7.2 1.2 copy.60
  8.4 0.8 copy.61
  9.2 7.3 %all-to-all-start = ((bf16[1,4,32,4,256]{4,3,1,0,2:T(4,128)(2,1)}), bf16[1,4,32,4,256]{4,3,1,0,2:T(4,128)(2,1)S(1)}, u32[]{:S(2)}, u32[]{:S(2)}) async-start(bf16[1,4,32,4,256]{4,3,1,0,2:T(4,128)(2,1)} %copy.61), calls=%async_computation | async-start | bytes 524288 | tf_op jit(solution)/shard_map/all_to_all | solution.py:172
  16.6 1.0 fusion.21
  17.6 12.0 %all-gather = bf16[8,4,128]{2,1,0:T(4,128)(2,1)S(1)} all-gather(bf16[1,4,128]{2,1,0:T(4,128)(2,1)S(1)} %fusion.21), channel_id=1, replica_groups=mesh['row'=4,'col'=8] {'col'}, dimensions={0}, use_global_device_ids=true | all-gather | bytes 9216 | tf_op jit(solution)/shard_map/all_gather | solution.py:213
  29.6 1.0 fusion.22
  30.6 8.9 %all-gather.1 = bf16[8,4,128]{2,1,0:T(4,128)(2,1)S(1)} all-gather(bf16[1,4,128]{2,1,0:T(4,128)(2,1)S(1)} %fusion.22), channel_id=1, replica_groups=mesh['row'=4,'col'=8] {'col'}, dimensions={0}, use_global_device_ids=true | all-gather | bytes 9216 | tf_op jit(solution)/shard_map/all_gather | solution.py:214
  39.6 10.2 %all-reduce = (bf16[16,128]{1,0:T(8,128)(2,1)S(1)}, bf16[16,128]{1,0:T(8,128)(2,1)S(1)}) all-reduce(bf16[16,128]{1,0:T(8,128)(2,1)S(1)} %dynamic-slice_select_fusion.1, bf16[16,128]{1,0:T(8,128)(2,1)S(1)} %dynamic-slice_select_fusion), channel_id=1, replica_groups=mesh['row'=4,'col'=8] {'row'}, use_global_device_ids=true, to_apply=%region_6.7 | all-reduce | flops 4096 | bytes 16384 | tf_op jit(solution)/shard_map/psum | solution.py:14
  49.8 0.1 sub.146
  49.9 0.1 sub.147
  49.9 0.1 sub.145
  50.0 0.1 sub.136
  50.1 0.1 sub.137
  50.2 0.1 sub.138
  50.3 0.7 broadcast_add_fusion
  51.0 0.3 fusion.31
  51.3 0.1 div.73
  51.4 0.5 multiply_reduce_fusion.3
  51.9 0.1 rsqrt.46
  52.0 0.1 convert_bitcast_fusion
  52.2 0.2 reshape.311
  52.4 0.3 convolution_convert_fusion.1
  52.7 0.4 reshape.299
  53.2 0.3 convolution_convert_fusion
  53.5 0.4 reshape.300
  53.9 2.1 %fusion.24 = f32[4,8,128,128]{2,3,1,0:T(8,128)} fusion(bf16[128,4,8,32]{3,2,1,0:T(8,128)(2,1)S(1)} %reshape.300, bf16[128,4,8,32]{3,2,1,0:T(8,128)(2,1)S(1)} %reshape.299), kind=kOutput, calls=%fused_computation.44 | convolution fusion | flops 33554432 | bytes 2621440 | tf_op jit(solution)/shard_map/sihd,tihd->ihst/dot_general | solution.py:52
  56.1 1.2 fusion.72
  57.3 0.3 convolution_convert_fusion.2
  57.7 0.4 reshape.298
  58.1 3.3 %convolution_bitcast_fusion = f32[128,4,8,32]{0,3,2,1:T(8,128)} fusion(bf16[128,4,8,32]{3,2,1,0:T(8,128)(2,1)S(1)} %reshape.298, f32[4,8,128]{2,1,0:T(8,128)S(1)} %fusion.72, f32[4,8,128,128]{2,3,1,0:T(8,128)} %fusion.24), kind=kOutput, calls=%fused_computation.16 | convolution fusion | flops 35655808 | bytes 2899968 | tf_op jit(solution)/shard_map/ihst,tihd->sihd/dot_general | solution.py:56
  61.4 2.9 %copy.66 = f32[128,4,8,32]{3,2,1,0:T(8,128)S(1)} copy(f32[128,4,8,32]{0,3,2,1:T(8,128)} %convolution_bitcast_fusion) | data formatting | bytes 1048576 | tf_op jit(solution)/shard_map/ihst,tihd->sihd/transpose | solution.py:56
  64.3 1.4 reshape.301
  65.7 1.6 fusion.77
  67.4 0.2 multiply_reduce_fusion.2
  67.7 0.9 fusion.78
  68.6 0.2 multiply_reduce_fusion.1
  68.9 0.2 multiply_convert_fusion.2
  69.1 0.2 convolution_convert_fusion.4
  69.3 0.1 copy.67
  69.4 0.1 copy.68
  69.5 14.4 %all_gather.14 = bf16[128,32,32]{0,2,1:T(8,128)(2,1)S(1)} all-gather(bf16[128,4,32]{0,2,1:T(8,128)(2,1)S(1)} %copy.68), channel_id=1, replica_groups=mesh['row'=4,'col'=8] {'col'}, dimensions={1}, use_global_device_ids=true | all-gather | bytes 294912 | tf_op jit(solution)/shard_map/all_gather | solution.py:211
  83.9 0.7 select_bitcast_fusion
  84.6 0.2 convolution_convert_fusion.3
  84.7 0.1 copy.69
  84.9 0.1 copy.70
  85.0 14.2 %all_gather.15 = bf16[128,32,32]{0,2,1:T(8,128)(2,1)S(1)} all-gather(bf16[128,4,32]{0,2,1:T(8,128)(2,1)S(1)} %copy.70), channel_id=1, replica_groups=mesh['row'=4,'col'=8] {'col'}, dimensions={1}, use_global_device_ids=true | all-gather | bytes 294912 | tf_op jit(solution)/shard_map/all_gather | solution.py:212
  99.2 0.7 select_bitcast_fusion.1
  100.0 0.1 copy.72
  100.1 0.8 convert_element_type.150
  100.9 39.5 %all-reduce.4.cloned.1.call-done = (bf16[16,32,128]{2,1,0:T(8,128)(2,1)}, bf16[16,32,128]{2,1,0:T(8,128)(2,1)}) async-done(((bf16[16,32,128]{2,1,0:T(8,128)(2,1)}, bf16[16,32,128]{2,1,0:T(8,128)(2,1)}), (bf16[16,32,128]{2,1,0:T(8,128)(2,1)}, bf16[16,32,128]{2,1,0:T(8,128)(2,1)})) %all-reduce.4.cloned.1.call-update) | async-done | bytes 262160 | tf_op jit(solution)/shard_map/psum | solution.py:14
  140.4 4.1 %fusion.2 = bf16[16,32,32,32]{3,2,1,0:T(8,128)(2,1)} fusion(bf16[128,32,32]{0,2,1:T(8,128)(2,1)S(1)} %all_gather.15, bf16[16,32,128]{2,1,0:T(8,128)(2,1)} %get-tuple-element.65), kind=kOutput, calls=%fused_computation.4 | convolution fusion | flops 135266304 | bytes 1441792 | tf_op jit(solution)/shard_map/while/body/eval_jaxpr/dot_general | solution.py:100
  144.5 6.2 %convert_element_type.168 = bf16[512,1024]{1,0:T(8,128)(2,1)S(1)} reshape(bf16[16,32,32,32]{3,2,1,0:T(8,128)(2,1)} %fusion.2) | data formatting | bytes 2097152 | tf_op jit(solution)/shard_map/while/body/eval_jaxpr/convert_element_type | solution.py:111
  150.7 0.5 fusion.83
  151.2 0.3 fusion.80
  151.6 3.2 %fusion.1 = bf16[32,16,32,32]{3,2,1,0:T(8,128)(2,1)} fusion(bf16[128,32,32]{0,2,1:T(8,128)(2,1)S(1)} %all_gather.14, bf16[16,32,128]{2,1,0:T(8,128)(2,1)S(1)} %copy-done.6), kind=kOutput, calls=%fused_computation.3 | convolution fusion | flops 135266304 | bytes 1441792 | tf_op jit(solution)/shard_map/while/body/eval_jaxpr/dot_general | solution.py:100
  154.8 6.2 %convert_element_type.160 = bf16[512,1024]{1,0:T(8,128)(2,1)S(1)} reshape(bf16[32,16,32,32]{3,2,1,0:T(8,128)(2,1)} %fusion.1) | data formatting | bytes 2097152 | tf_op jit(solution)/shard_map/while/body/eval_jaxpr/convert_element_type | solution.py:111
  161.0 0.4 fusion.81
  161.4 0.4 fusion.79
  161.8 0.2 multiply_reduce_fusion.5
  162.1 0.6 fusion.19
  162.7 0.5 fusion.20
  163.2 0.2 fusion.84
  163.4 0.2 fusion.82
  163.6 0.8 fusion.34
  (61 shorter events, 0.4 us)
Async XLA Ops:
  7.2 60.5 %copy-start = (bf16[1024,256]{1,0:T(8,128)(2,1)S(1)}, bf16[1024,256]{1,0:T(8,128)(2,1)}, u32[]{:S(2)}) copy-start(bf16[1024,256]{1,0:T(8,128)(2,1)} %param.26) | copy-start | bytes 1572868
  9.2 43.2 %copy-start.3 = (bf16[256,256]{1,0:T(8,128)(2,1)S(1)}, bf16[256,256]{1,0:T(8,128)(2,1)}, u32[]{:S(2)}) copy-start(bf16[256,256]{1,0:T(8,128)(2,1)} %param.20) | copy-start | bytes 393220
  9.2 41.8 %all-to-all-start = ((bf16[1,4,32,4,256]{4,3,1,0,2:T(4,128)(2,1)}), bf16[1,4,32,4,256]{4,3,1,0,2:T(4,128)(2,1)S(1)}, u32[]{:S(2)}, u32[]{:S(2)}) async-start(bf16[1,4,32,4,256]{4,3,1,0,2:T(4,128)(2,1)} %copy.61), calls=%async_computation | async-start | bytes 524288 | tf_op jit(solution)/shard_map/all_to_all | solution.py:172
  16.5 123.8 %all-reduce.4.cloned.1.call-start = ((), (), s32[]{:S(2)}) async-start(), calls=%async_computation.1 | async-start | bytes 524288 | tf_op jit(solution)/shard_map/psum | solution.py:14
  51.9 1.3 copy-start.4
  56.1 1.3 copy-start.5
  61.4 4.3 %copy-start.13 = (bf16[256,256]{1,0:T(8,128)(2,1)S(1)}, bf16[256,256]{1,0:T(8,128)(2,1)}, u32[]{:S(2)}) copy-start(bf16[256,256]{1,0:T(8,128)(2,1)} %param.24) | copy-start | bytes 393220
  61.4 4.3 %copy-start.14 = (bf16[256,256]{1,0:T(8,128)(2,1)S(1)}, bf16[256,256]{1,0:T(8,128)(2,1)}, u32[]{:S(2)}) copy-start(bf16[256,256]{1,0:T(8,128)(2,1)} %param.23) | copy-start | bytes 393220
  65.7 1.9 %copy-start.12 = (bf16[256,1024]{1,0:T(8,128)(2,1)S(1)}, bf16[256,1024]{1,0:T(8,128)(2,1)}, u32[]{:S(2)}) copy-start(bf16[256,1024]{1,0:T(8,128)(2,1)} %param.25) | copy-start | bytes 1572868
  67.6 1.4 copy-start.10
  68.6 16.0 %copy-start.11 = (bf16[256,32]{0,1:T(8,128)(2,1)S(1)}, bf16[256,32]{0,1:T(8,128)(2,1)}, u32[]{:S(2)}) copy-start(bf16[256,32]{0,1:T(8,128)(2,1)} %param.28) | copy-start | bytes 49156
  68.6 31.3 %copy-start.1 = (f32[16,32,128]{2,1,0:T(8,128)S(1)}, f32[16,32,128]{2,1,0:T(8,128)}, u32[]{:S(2)}) copy-start(f32[16,32,128]{2,1,0:T(8,128)} %broadcast_add_fusion) | copy-start | bytes 786436
  144.5 6.2 %copy-start.2 = (bf16[1024,128]{1,0:T(8,128)(2,1)S(1)}, bf16[1024,128]{1,0:T(8,128)(2,1)}, u32[]{:S(2)}) copy-start(bf16[1024,128]{1,0:T(8,128)(2,1)} %param.29) | copy-start | bytes 786436
  144.5 6.7 %copy-start.8 = (bf16[65,128]{1,0:T(8,128)(2,1)S(1)}, bf16[65,128]{1,0:T(8,128)(2,1)}, u32[]{:S(2)}) copy-start(bf16[65,128]{1,0:T(8,128)(2,1)} %param.32) | copy-start | bytes 49924
  150.7 0.9 copy-start.6
  161.0 1.1 copy-start.15
  161.0 1.1 copy-start.16
  161.0 2.2 %copy-start.9 = (bf16[128,64]{0,1:T(8,128)(2,1)S(1)}, bf16[128,64]{0,1:T(8,128)(2,1)}, u32[]{:S(2)}) copy-start(bf16[128,64]{0,1:T(8,128)(2,1)} %param.35) | copy-start | bytes 49156
  163.2 1.2 copy-start.7
Sparse Core Ops, SparseCore 0:
  100.0 40.2 all-reduce.3
where the time goes:
time: 172 us; the launch traced here: 171 us
  blocking collectives  59.7 us (35%)
  waiting for transfers between devices  39.5 us (23%)
  matrix products  22.8 us (13%)
  local copies, waits for them, and re-layouts  22.4 us (13%)
  between operations  14.6 us (8%)
  starting transfers between devices  7.37 us (4%)
  other arithmetic  4.9 us (3%)
    psum x1, waiting for transfers between devices, spread_2(): return lax.psum(block, axis)  39.5 us
    all_gather x1, blocking collectives, shards(): lax.all_gather(left_opm, 'col', axis=1, tiled=True)  14.4 us
    all_gather x1, blocking collectives, shards(): lax.all_gather(right_opm, 'col', axis=1, tiled=True)  14.2 us
    convert_element_type x2, local copies, waits for them, and re-layouts, one_block(): outer = (outer / count_seq).astype(jnp.bfloat16)  12.4 us
    all_gather x1, blocking collectives, shards(): lax.all_gather(left_pair, 'col', axis=0, tiled=True)  12 us
    psum x1, blocking collectives, spread_2(): return lax.psum(block, axis)  10.2 us
    all_gather x1, blocking collectives, shards(): lax.all_gather(right_pair, 'col', axis=0, tiled=True)  8.93 us
    all_to_all x1, starting transfers between devices, shards(): lax.all_to_all(fragment_collection, ('row', 'col'), split_axis=2, concat_...  7.33 us
  transfers between devices with their start and end apart: 2, of which 1 were waited for; matrix products, arithmetic and copies ran while one was open for 2% of the time, Pallas kernels for 0%

commit v1 on v0

--- a/solution.py
+++ b/solution.py
@@ -11,7 +11,7 @@
 
 def spread_2(block, axis, source):
     block = jnp.where(lax.axis_index(axis) == source, block, jnp.zeros_like(block))
-    return lax.psum(block, axis)
+    return jnp.sum(lax.all_gather(block, axis), axis=0)
 
 
 def standardize_features(values):

time: 172 us -> 154 us (0.90)
  waiting for transfers between devices: 39.5 us -> 0.01 us
  blocking collectives: 59.7 us -> 87.4 us
  between operations: 14.6 us -> 1.2 us
  local copies, waits for them, and re-layouts: 22.4 us -> 28.5 us
    psum x1 -> x0, waiting for transfers between devices: 39.5 us -> none  [spread_2(): return lax.psum(block, axis)]
    all_gather x0 -> x4, blocking collectives: none -> 36.7 us  [spread_2(): return jnp.sum(lax.all_gather(block, axis), axis=0)]
    psum x1 -> x0, blocking collectives: 10.2 us -> none  [spread_2(): return lax.psum(block, axis)]
    all_gather x0 -> x2, local copies, waits for them, and re-layouts: none -> 3.95 us  [spread_2(): return jnp.sum(lax.all_gather(block, axis), axis=0)]
    all_gather x1, blocking collectives: 8.93 us -> 12 us  [shards(): lax.all_gather(right_pair, 'col', axis=0, tiled=True)]
    all_gather x1, blocking collectives: 12 us -> 8.98 us  [shards(): lax.all_gather(left_pair, 'col', axis=0, tiled=True)]
  transfers between devices with their start and end apart: 2 -> 1, of which waited for: 1 -> 0; matrix products, arithmetic and copies ran while one was open for 2% -> 3% of each run, Pallas kernels for 0% -> 0%
where the time goes in v1:
time: 154 us; the launch traced here: 153 us
  blocking collectives  87.4 us (57%)
  local copies, waits for them, and re-layouts  28.5 us (19%)
  matrix products  22.9 us (15%)
  starting transfers between devices  7.33 us (5%)
  other arithmetic  6.06 us (4%)
    all_gather x4, blocking collectives, spread_2(): return jnp.sum(lax.all_gather(block, axis), axis=0)  36.7 us
    all_gather x1, blocking collectives, shards(): lax.all_gather(left_opm, 'col', axis=1, tiled=True)  15.4 us
    all_gather x1, blocking collectives, shards(): lax.all_gather(right_opm, 'col', axis=1, tiled=True)  14.3 us
    convert_element_type x2, local copies, waits for them, and re-layouts, one_block(): outer = (outer / count_seq).astype(jnp.bfloat16)  12.4 us
    all_gather x1, blocking collectives, shards(): lax.all_gather(right_pair, 'col', axis=0, tiled=True)  12 us
    all_gather x1, blocking collectives, shards(): lax.all_gather(left_pair, 'col', axis=0, tiled=True)  8.98 us
    dot_general x2, matrix products, one_block(): lax.dot_general(a_blk.reshape(count_seq, step_rows * factor), flat_v, (((...  7.34 us
    all_to_all x1, starting transfers between devices, shards(): lax.all_to_all(fragment_collection, ('row', 'col'), split_axis=2, concat_...  7.33 us
  transfers between devices with their start and end apart: 1, of which 0 were waited for; matrix products, arithmetic and copies ran while one was open for 3% of the time, Pallas kernels for 0%

profile of v1, /device:TPU:0, one launch (start us, length us, event | category | flops | bytes accessed | tf_op | source)
XLA Modules:
  0.0 153.4 jit_solution(1609138964029612331)
XLA Ops:
  0.6 1.2 copy.61
  1.9 0.8 copy.62
  2.7 7.3 %all-to-all-start = ((bf16[1,4,32,4,256]{4,3,1,0,2:T(4,128)(2,1)}), bf16[1,4,32,4,256]{4,3,1,0,2:T(4,128)(2,1)S(1)}, u32[]{:S(2)}, u32[]{:S(2)}) async-start(bf16[1,4,32,4,256]{4,3,1,0,2:T(4,128)(2,1)} %copy.62), calls=%async_computation | async-start | bytes 524288 | tf_op jit(solution)/shard_map/all_to_all | solution.py:172
  10.0 1.0 fusion.22
  11.0 12.0 %all-gather.5 = bf16[8,4,128]{2,1,0:T(4,128)(2,1)S(1)} all-gather(bf16[1,4,128]{2,1,0:T(4,128)(2,1)S(1)} %fusion.22), channel_id=1, replica_groups=mesh['row'=4,'col'=8] {'col'}, dimensions={0}, use_global_device_ids=true | all-gather | bytes 9216 | tf_op jit(solution)/shard_map/all_gather | solution.py:214
  23.0 1.0 fusion.21
  24.0 9.0 %all-gather.4 = bf16[8,4,128]{2,1,0:T(4,128)(2,1)S(1)} all-gather(bf16[1,4,128]{2,1,0:T(4,128)(2,1)S(1)} %fusion.21), channel_id=1, replica_groups=mesh['row'=4,'col'=8] {'col'}, dimensions={0}, use_global_device_ids=true | all-gather | bytes 9216 | tf_op jit(solution)/shard_map/all_gather | solution.py:213
  33.3 8.3 %all-gather.2 = bf16[64,128]{1,0:T(8,128)(2,1)S(1)} all-gather(bf16[16,128]{1,0:T(8,128)(2,1)S(1)} %dynamic-slice_select_fusion.2), channel_id=4, replica_groups=mesh['row'=4,'col'=8] {'row'}, dimensions={0}, use_global_device_ids=true | all-gather | bytes 20480 | tf_op jit(solution)/shard_map/all_gather | solution.py:14
  41.7 8.1 %all-gather = bf16[64,128]{1,0:T(8,128)(2,1)S(1)} all-gather(bf16[16,128]{1,0:T(8,128)(2,1)S(1)} %dynamic-slice_select_fusion.3), channel_id=2, replica_groups=mesh['row'=4,'col'=8] {'row'}, dimensions={0}, use_global_device_ids=true | all-gather | bytes 20480 | tf_op jit(solution)/shard_map/all_gather | solution.py:14
  49.9 0.8 copy.75
  50.9 0.7 broadcast_add_fusion.1
  51.7 0.1 convert_bitcast_fusion
  51.8 0.2 reshape.313
  52.0 0.3 fusion.31
  52.3 0.1 div.73
  52.4 0.5 multiply_reduce_fusion.3
  52.9 0.1 rsqrt.46
  53.0 0.3 convolution_convert_fusion
  53.4 0.4 reshape.302
  53.8 0.3 convolution_convert_fusion.1
  54.1 0.4 reshape.301
  54.6 1.2 fusion.72
  55.8 2.1 %fusion.24 = f32[4,8,128,128]{2,3,1,0:T(8,128)} fusion(bf16[128,4,8,32]{3,2,1,0:T(8,128)(2,1)S(1)} %reshape.302, bf16[128,4,8,32]{3,2,1,0:T(8,128)(2,1)S(1)} %reshape.301), kind=kOutput, calls=%fused_computation.44 | convolution fusion | flops 33554432 | bytes 2621440 | tf_op jit(solution)/shard_map/sihd,tihd->ihst/dot_general | solution.py:52
  58.0 0.3 convolution_convert_fusion.2
  58.3 0.4 reshape.300
  58.8 3.3 %convolution_bitcast_fusion = f32[128,4,8,32]{0,3,2,1:T(8,128)} fusion(bf16[128,4,8,32]{3,2,1,0:T(8,128)(2,1)S(1)} %reshape.300, f32[4,8,128]{2,1,0:T(8,128)S(1)} %fusion.72, f32[4,8,128,128]{2,3,1,0:T(8,128)} %fusion.24), kind=kOutput, calls=%fused_computation.16 | convolution fusion | flops 35655808 | bytes 2899968 | tf_op jit(solution)/shard_map/ihst,tihd->sihd/dot_general | solution.py:56
  62.1 2.9 %copy.67 = f32[128,4,8,32]{3,2,1,0:T(8,128)S(1)} copy(f32[128,4,8,32]{0,3,2,1:T(8,128)} %convolution_bitcast_fusion) | data formatting | bytes 1048576 | tf_op jit(solution)/shard_map/ihst,tihd->sihd/transpose | solution.py:56
  65.0 1.4 reshape.303
  66.4 1.6 %fusion.77 = (f32[512]{0:T(512)S(1)}, f32[512,256]{1,0:T(8,128)S(1)}) fusion(f32[512,256]{1,0:T(8,128)S(1)} %reshape.313, bf16[256,256]{1,0:T(8,128)(2,1)S(1)} %copy-done.16, f32[512,256]{1,0:T(8,128)} %reshape.303, bf16[256,256]{1,0:T(8,128)(2,1)S(1)} %copy-done.17, f32[512]{0:T(512)S(1)} %rsqrt.46, f32[512]{0:T(512)S(1)} %div.73), kind=kOutput, calls=%fused_computation.109 | convolution fusion | flops 135527936 | bytes 1841152 | tf_op jit(solution)/shard_map/dot_general | solution.py:60
  68.0 0.2 multiply_reduce_fusion.2
  68.3 0.9 fusion.78
  69.3 0.2 multiply_reduce_fusion.1
  69.5 0.2 multiply_convert_fusion.2
  69.7 0.8 convert_element_type.164
  70.5 0.2 convolution_convert_fusion.4
  70.7 0.1 copy.68
  70.9 15.4 %all_gather.40 = bf16[128,32,32]{0,2,1:T(8,128)(2,1)} all-gather(bf16[128,4,32]{0,2,1:T(8,128)(2,1)S(1)} %copy.69), channel_id=1, replica_groups=mesh['row'=4,'col'=8] {'col'}, dimensions={1}, use_global_device_ids=true | all-gather | bytes 294912 | tf_op jit(solution)/shard_map/all_gather | solution.py:211
  86.4 0.2 convolution_convert_fusion.3
  86.6 0.1 copy.70
  86.8 14.3 %all_gather.41 = bf16[128,32,32]{0,2,1:T(8,128)(2,1)S(1)} all-gather(bf16[128,4,32]{0,2,1:T(8,128)(2,1)S(1)} %copy.71), channel_id=1, replica_groups=mesh['row'=4,'col'=8] {'col'}, dimensions={1}, use_global_device_ids=true | all-gather | bytes 294912 | tf_op jit(solution)/shard_map/all_gather | solution.py:212
  101.1 9.3 %all-gather.1 = bf16[512,16,32]{0,2,1:T(8,128)(2,1)S(1)} all-gather(bf16[128,16,32]{0,2,1:T(8,128)(2,1)S(1)} %dynamic-slice_select_fusion.1), channel_id=3, replica_groups=mesh['row'=4,'col'=8] {'row'}, dimensions={0}, use_global_device_ids=true | all-gather | bytes 655360 | tf_op jit(solution)/shard_map/all_gather | solution.py:14
  110.4 2.0 %copy.87 = bf16[512,16,32]{2,1,0:T(8,128)(2,1)S(1)} copy(bf16[512,16,32]{0,2,1:T(8,128)(2,1)S(1)} %all-gather.1) | data formatting | bytes 1048576 | tf_op jit(solution)/shard_map/all_gather | solution.py:14
  112.4 0.8 reduce_sum.159
  113.2 0.4 copy.73
  113.6 0.9 dynamic-slice_select_fusion
  114.6 4.1 %fusion.1 = bf16[32,16,32,32]{3,2,1,0:T(8,128)(2,1)} fusion(bf16[128,32,32]{0,2,1:T(8,128)(2,1)} %all_gather.40, bf16[128,16,32]{0,2,1:T(8,128)(2,1)S(1)} %copy.73), kind=kOutput, calls=%fused_computation.3 | convolution fusion | flops 135266304 | bytes 1441792 | tf_op jit(solution)/shard_map/while/body/eval_jaxpr/dot_general | solution.py:100
  118.7 6.2 %convert_element_type.174 = bf16[512,1024]{1,0:T(8,128)(2,1)S(1)} reshape(bf16[32,16,32,32]{3,2,1,0:T(8,128)(2,1)} %fusion.1) | data formatting | bytes 2097152 | tf_op jit(solution)/shard_map/while/body/eval_jaxpr/convert_element_type | solution.py:111
  125.0 0.4 fusion.81
  125.4 0.4 fusion.79
  125.8 0.2 multiply_reduce_fusion.5
  126.1 0.4 copy-done.3
  126.5 10.9 %all-gather.3 = bf16[512,16,32]{0,2,1:T(8,128)(2,1)S(1)} all-gather(bf16[128,16,32]{0,2,1:T(8,128)(2,1)S(1)} %dynamic-slice_select_fusion), channel_id=5, replica_groups=mesh['row'=4,'col'=8] {'row'}, dimensions={0}, use_global_device_ids=true | all-gather | bytes 655360 | tf_op jit(solution)/shard_map/all_gather | solution.py:14
  137.4 2.0 %copy.88 = bf16[512,16,32]{2,1,0:T(8,128)(2,1)S(1)} copy(bf16[512,16,32]{0,2,1:T(8,128)(2,1)S(1)} %all-gather.3) | data formatting | bytes 1048576 | tf_op jit(solution)/shard_map/all_gather | solution.py:14
  139.4 0.8 reduce_sum.163
  140.2 0.4 copy.77
  140.7 3.2 %fusion.2 = bf16[16,32,32,32]{3,2,1,0:T(8,128)(2,1)} fusion(bf16[128,32,32]{0,2,1:T(8,128)(2,1)S(1)} %all_gather.41, bf16[128,16,32]{0,2,1:T(8,128)(2,1)S(1)} %copy.77), kind=kOutput, calls=%fused_computation.4 | convolution fusion | flops 135266304 | bytes 1441792 | tf_op jit(solution)/shard_map/while/body/eval_jaxpr/dot_general | solution.py:100
  143.9 6.2 %convert_element_type.182 = bf16[512,1024]{1,0:T(8,128)(2,1)S(1)} reshape(bf16[16,32,32,32]{3,2,1,0:T(8,128)(2,1)} %fusion.2) | data formatting | bytes 2097152 | tf_op jit(solution)/shard_map/while/body/eval_jaxpr/convert_element_type | solution.py:111
  150.1 0.5 fusion.83
  150.6 0.3 fusion.80
  151.1 0.5 fusion.20
  151.6 0.6 fusion.19
  152.2 0.2 fusion.82
  152.4 0.2 fusion.84
  152.6 0.8 fusion.34
  (75 shorter events, 1.2 us)
Async XLA Ops:
  0.6 67.7 %copy-start = (bf16[1024,256]{1,0:T(8,128)(2,1)S(1)}, bf16[1024,256]{1,0:T(8,128)(2,1)}, u32[]{:S(2)}) copy-start(bf16[1024,256]{1,0:T(8,128)(2,1)} %param.26) | copy-start | bytes 1572868
  2.7 49.0 %all-to-all-start = ((bf16[1,4,32,4,256]{4,3,1,0,2:T(4,128)(2,1)}), bf16[1,4,32,4,256]{4,3,1,0,2:T(4,128)(2,1)S(1)}, u32[]{:S(2)}, u32[]{:S(2)}) async-start(bf16[1,4,32,4,256]{4,3,1,0,2:T(4,128)(2,1)} %copy.62), calls=%async_computation | async-start | bytes 524288 | tf_op jit(solution)/shard_map/all_to_all | solution.py:172
  41.6 11.4 %copy-start.7 = (bf16[256,256]{1,0:T(8,128)(2,1)S(1)}, bf16[256,256]{1,0:T(8,128)(2,1)}, u32[]{:S(2)}) copy-start(bf16[256,256]{1,0:T(8,128)(2,1)} %param.21) | copy-start | bytes 393220
  51.8 2.0 %copy-start.8 = (bf16[256,256]{1,0:T(8,128)(2,1)S(1)}, bf16[256,256]{1,0:T(8,128)(2,1)}, u32[]{:S(2)}) copy-start(bf16[256,256]{1,0:T(8,128)(2,1)} %param.20) | copy-start | bytes 393220
  55.8 2.1 %copy-start.9 = (bf16[256,256]{1,0:T(8,128)(2,1)S(1)}, bf16[256,256]{1,0:T(8,128)(2,1)}, u32[]{:S(2)}) copy-start(bf16[256,256]{1,0:T(8,128)(2,1)} %param.22) | copy-start | bytes 393220
  62.1 4.3 %copy-start.16 = (bf16[256,256]{1,0:T(8,128)(2,1)S(1)}, bf16[256,256]{1,0:T(8,128)(2,1)}, u32[]{:S(2)}) copy-start(bf16[256,256]{1,0:T(8,128)(2,1)} %param.24) | copy-start | bytes 393220
  62.1 4.3 %copy-start.17 = (bf16[256,256]{1,0:T(8,128)(2,1)S(1)}, bf16[256,256]{1,0:T(8,128)(2,1)}, u32[]{:S(2)}) copy-start(bf16[256,256]{1,0:T(8,128)(2,1)} %param.23) | copy-start | bytes 393220
  66.4 1.9 %copy-start.15 = (bf16[256,1024]{1,0:T(8,128)(2,1)S(1)}, bf16[256,1024]{1,0:T(8,128)(2,1)}, u32[]{:S(2)}) copy-start(bf16[256,1024]{1,0:T(8,128)(2,1)} %param.25) | copy-start | bytes 1572868
  68.3 2.2 %copy-start.13 = (bf16[256,32]{0,1:T(8,128)(2,1)S(1)}, bf16[256,32]{0,1:T(8,128)(2,1)}, u32[]{:S(2)}) copy-start(bf16[256,32]{0,1:T(8,128)(2,1)} %param.27) | copy-start | bytes 49156
  69.3 17.1 %copy-start.14 = (bf16[256,32]{0,1:T(8,128)(2,1)S(1)}, bf16[256,32]{0,1:T(8,128)(2,1)}, u32[]{:S(2)}) copy-start(bf16[256,32]{0,1:T(8,128)(2,1)} %param.28) | copy-start | bytes 49156
  118.7 6.2 %copy-start.5 = (bf16[1024,128]{1,0:T(8,128)(2,1)S(1)}, bf16[1024,128]{1,0:T(8,128)(2,1)}, u32[]{:S(2)}) copy-start(bf16[1024,128]{1,0:T(8,128)(2,1)} %param.29) | copy-start | bytes 786436
  118.7 6.7 %copy-start.2 = (f32[32,16,128]{2,1,0:T(8,128)S(1)}, f32[32,16,128]{2,1,0:T(8,128)}, u32[]{:S(2)}) copy-start(f32[32,16,128]{2,1,0:T(8,128)} %broadcast_add_fusion.1) | copy-start | bytes 786436
  118.7 6.7 %copy-start.11 = (bf16[65,128]{1,0:T(8,128)(2,1)S(1)}, bf16[65,128]{1,0:T(8,128)(2,1)}, u32[]{:S(2)}) copy-start(bf16[65,128]{1,0:T(8,128)(2,1)} %param.32) | copy-start | bytes 49924
  125.8 0.7 copy-start.3
  143.8 6.2 %copy-start.6 = (bf16[1024,128]{1,0:T(8,128)(2,1)S(1)}, bf16[1024,128]{1,0:T(8,128)(2,1)}, u32[]{:S(2)}) copy-start(bf16[1024,128]{1,0:T(8,128)(2,1)} %param.29) | copy-start | bytes 786436
  143.8 6.8 %copy-start.1 = (f32[512,128]{0,1:T(8,128)S(1)}, f32[512,128]{0,1:T(8,128)}, u32[]{:S(2)}) copy-start(f32[512,128]{0,1:T(8,128)} %copy.75) | copy-start | bytes 786436
  150.1 1.0 copy-start.4
  150.1 1.0 copy-start.18
  150.1 1.0 copy-start.19
  150.1 2.1 %copy-start.12 = (bf16[128,64]{0,1:T(8,128)(2,1)S(1)}, bf16[128,64]{0,1:T(8,128)(2,1)}, u32[]{:S(2)}) copy-start(bf16[128,64]{0,1:T(8,128)(2,1)} %param.35) | copy-start | bytes 49156
  151.6 1.8 %copy-start.10 = (bf16[512,128]{1,0:T(8,128)(2,1)}, bf16[512,128]{1,0:T(8,128)(2,1)S(1)}, u32[]{:S(2)}) copy-start(bf16[512,128]{1,0:T(8,128)(2,1)S(1)} %fusion.20) | copy-start | bytes 393220
